TPU v7x, 32 devices: a whole 2x2x4 slice. The times are simulated.
32 devices in a mesh: work: 8 (over z, y), firm: 4 (over x, core).
Axes of the slice: x: 2, y: 2, z: 4, core: 2. Of those that a mesh axis runs over, the one named last changes fastest.
Arguments:
- worker_feat: bfloat16 [64, 16384], P('firm', 'work'), may hold values from -4 to 4
- firm_feat: bfloat16 [64, 16384], P('work', 'firm'), may hold values from -1.75 to 1.75
- worker_pot: float32 [16384], P('work'), may hold values from -1 to 1
- firm_pot: float32 [16384], P('firm'), may hold values from -1 to 1
- worker_caps: int32 [16384], P('work'), may hold values from 1 to 5
- firm_caps: int32 [16384], P('firm'), may hold values from 1 to 5
Outputs:
- step_workers: float32 [16384], P('work')
- step_firms: float32 [16384], P('firm')
All inputs are finite; a program needn't handle non-finite values.
Results may differ from a plain program's by a relative error of at most 0.0003.
Values may be sent and summed in bfloat16 or wider, within the bound.
A program may use at most 64 MiB of HBM per device.

v0:
```python
import math
import jax
import jax.numpy as jnp
from jax import lax
from jax.sharding import PartitionSpec as P

ITERS = 4


def body(worker_feat, firm_feat, worker_pot, firm_pot, worker_caps, firm_caps):
    wfeat = lax.all_gather(worker_feat, "firm", axis=0, tiled=True)
    ffeat = lax.all_gather(firm_feat, "work", axis=0, tiled=True)
    rows_here = wfeat.shape[1]
    cols_here = ffeat.shape[1]
    inverse = 1.0 / (cols_here * lax.axis_size("firm"))
    scale = 1.0 / math.sqrt(wfeat.shape[0])
    width = 256
    blocks = cols_here // width
    first_firm = lax.axis_index("firm") == 0
    first_work = lax.axis_index("work") == 0

    def kernel_pass(vec_u, vec_v):

        def step(rows_acc, index):
            start = index * width
            feat_blk = lax.dynamic_slice_in_dim(ffeat, start, width, 1)
            pot_blk = lax.dynamic_slice_in_dim(firm_pot, start, width, 0)
            vec_blk = lax.dynamic_slice_in_dim(vec_v, start, width, 0)
            surplus = lax.dot_general(
                wfeat, feat_blk, (((0,), (0,)), ((), ())), preferred_element_type=jnp.float32
            )
            kernel = jnp.exp(surplus * scale - worker_pot[:, None] - pot_blk[None, :]) * inverse
            rows_acc = rows_acc + jnp.dot(kernel, vec_blk, precision=lax.Precision.HIGHEST)
            col_blk = jnp.dot(vec_u, kernel, precision=lax.Precision.HIGHEST)
            return (rows_acc, col_blk)

        rows_part, col_blocks = lax.scan(
            step, jnp.zeros((rows_here,), jnp.float32), jnp.arange(blocks, dtype=jnp.int32)
        )
        rows_full = lax.psum(rows_part, "firm")
        cols_part = col_blocks.reshape(cols_here)
        cols = lax.psum(cols_part, "work")
        return (rows_full, cols)

    row_total, col_total = kernel_pass(
        jnp.ones((rows_here,), jnp.float32), jnp.ones((cols_here,), jnp.float32)
    )
    diag_u = row_total + jnp.exp(-worker_pot)
    diag_v = col_total + jnp.exp(-firm_pot)
    rhs_u = diag_u - worker_caps.astype(jnp.float32)
    rhs_v = diag_v - firm_caps.astype(jnp.float32)

    def hessian(dir_u, dir_v):
        prod_u, prod_v = kernel_pass(dir_u, dir_v)
        return (diag_u * dir_u + prod_u, diag_v * dir_v + prod_v)

    def local_dot(left_u, left_v, right_u, right_v):
        part_u = jnp.where(first_firm, jnp.sum(left_u * right_u), 0.0)
        part_v = jnp.where(first_work, jnp.sum(left_v * right_v), 0.0)
        return part_u + part_v

    step_u = jnp.zeros_like(rhs_u)
    step_v = jnp.zeros_like(rhs_v)
    res_u, res_v = (rhs_u, rhs_v)

    def two_products(left_u, left_v, image_u, image_v):
        return lax.psum(
            (
                local_dot(left_u, left_v, left_u, left_v),
                local_dot(left_u, left_v, image_u, image_v),
            ),
            ("work", "firm"),
        )

    image_u, image_v = hessian(res_u, res_v)
    norm_now, product = two_products(res_u, res_v, image_u, image_v)
    alpha = norm_now / product
    dir_u, dir_v = (res_u, res_v)
    along_u, along_v = (image_u, image_v)
    for index in range(ITERS):
        step_u = step_u + alpha * dir_u
        step_v = step_v + alpha * dir_v
        if index + 1 < ITERS:
            res_u = res_u - alpha * along_u
            res_v = res_v - alpha * along_v
            image_u, image_v = hessian(res_u, res_v)
            norm_next, product = two_products(res_u, res_v, image_u, image_v)
            ratio = norm_next / norm_now
            alpha = norm_next / (product - ratio * norm_next / alpha)
            dir_u = res_u + ratio * dir_u
            dir_v = res_v + ratio * dir_v
            along_u = image_u + ratio * along_u
            along_v = image_v + ratio * along_v
            norm_now = norm_next
    return (step_u, step_v)


def solution(mesh):
    placed = (P("firm", "work"), P("work", "firm"), P("work"), P("firm"), P("work"), P("firm"))
    return jax.shard_map(
        body, mesh=mesh, in_specs=placed, out_specs=(P("work"), P("firm")), check_vma=False
    )
```

profile of v0, /device:TPU:12, one launch (start us, length us, event | category | flops | bytes accessed | tf_op | source)
XLA Modules:
  0.0 947.6 jit_solution(16463058012622074813)
XLA Ops:
  0.7 29.7 %all_gather.6 = bf16[64,4096]{1,0:T(8,128)(2,1)S(1)} all-gather(bf16[8,4096]{1,0:T(8,128)(2,1)} %param.17), channel_id=1, replica_groups=mesh['work'=8,'firm'=4] {'work'}, dimensions={0}, use_global_device_ids=true | all-gather | bytes 589824 | tf_op jit(solution)/shard_map/all_gather | solution.py:12
  30.3 6.0 all_gather.7
  36.3 103.3 %while.65 = (s32[]{:T(128)}, f32[2048]{0:T(1024)S(1)}, f32[16,256]{1,0:T(8,128)S(1)}, s32[16]{0:T(128)S(1)}, bf16[64,4096]{1,0:T(8,128)(2,1)S(1)}, /*index=5*/bf...) while((s32[]{:T(128)}, f32[2048]{0:T(1024)S(1)}, ...), condition=%wide.region_1.2_spmd.clone, body=%wide.region_0.1_spmd.clone.sunk | while | flops 81793032 | bytes 6633677 | solution.py:37
  139.6 32.1 %psum.127 = f32[4096]{0:T(1024)S(1)} all-reduce(f32[4096]{0:T(1024)S(1)} %bitcast.176), channel_id=1, replica_groups=mesh['work'=8,'firm'=4] {'work'}, use_global_device_ids=true, to_apply=%region_4.5 | all-reduce | flops 4096 | bytes 32768 | tf_op jit(solution)/shard_map/psum | solution.py:42
  172.5 5.8 psum.126
  179.0 104.5 %while.66 = (s32[]{:T(128)}, f32[2048]{0:T(1024)S(1)}, f32[16,256]{1,0:T(8,128)S(1)}, s32[16]{0:T(128)S(1)}, bf16[64,4096]{1,0:T(8,128)(2,1)S(1)}, /*index=5*/bf...) while((s32[]{:T(128)}, f32[2048]{0:T(1024)S(1)}, ...), condition=%wide.region_8.9_spmd.clone, body=%wide.region_7.8_spmd.clone.sunk | while | flops 81793032 | bytes 6644961 | solution.py:37
  183.7 1.7 fusion.134
  190.3 1.7 fusion.134
  196.8 1.7 fusion.134
  203.3 1.7 fusion.134
  209.8 1.7 fusion.134
  216.4 1.7 fusion.134
  222.9 1.7 fusion.134
  229.4 1.7 fusion.134
  283.4 6.7 psum.129
  291.5 36.0 %psum.130 = f32[4096]{0:T(1024)S(1)} all-reduce(f32[4096]{0:T(1024)S(1)} %bitcast.177), channel_id=1, replica_groups=mesh['work'=8,'firm'=4] {'work'}, use_global_device_ids=true, to_apply=%region_11.12 | all-reduce | flops 4096 | bytes 32768 | tf_op jit(solution)/shard_map/psum | solution.py:42
  330.2 43.5 %all-reduce.3 = (f32[]{:T(128)}, f32[]{:T(128)}) all-reduce(f32[]{:T(128)S(6)} %add.194, f32[]{:T(128)S(6)} %add.197), channel_id=1, replica_groups=mesh['work'=8,'firm'=4] {'work','firm'}, use_global_device_ids=true, to_apply=%region_6.7 | all-reduce | flops 2 | bytes 16 | tf_op jit(solution)/shard_map/psum | solution.py:67
  375.1 101.1 %while.67 = (s32[]{:T(128)}, f32[2048]{0:T(1024)S(1)}, f32[16,256]{1,0:T(8,128)S(1)}, s32[16]{0:T(128)S(1)}, bf16[64,4096]{1,0:T(8,128)(2,1)S(1)}, /*index=5*/bf...) while((s32[]{:T(128)}, f32[2048]{0:T(1024)S(1)}, ...), condition=%wide.region_18.19_spmd.clone, body=%wide.region_17.18_spmd.clone.sunk | while | flops 81793032 | bytes 6644961 | solution.py:37
  385.9 1.7 fusion.143
  417.5 1.7 fusion.143
  476.1 5.8 psum.133
  483.1 27.5 %psum.134 = f32[4096]{0:T(1024)S(1)} all-reduce(f32[4096]{0:T(1024)S(1)} %bitcast.178), channel_id=1, replica_groups=mesh['work'=8,'firm'=4] {'work'}, use_global_device_ids=true, to_apply=%region_21.22 | all-reduce | flops 4096 | bytes 32768 | tf_op jit(solution)/shard_map/psum | solution.py:42
  513.1 46.4 %all-reduce.2 = (f32[]{:T(128)}, f32[]{:T(128)}) all-reduce(f32[]{:T(128)S(6)} %add.198, f32[]{:T(128)S(6)} %add.201), channel_id=1, replica_groups=mesh['work'=8,'firm'=4] {'work','firm'}, use_global_device_ids=true, to_apply=%region_16.17 | all-reduce | flops 2 | bytes 16 | tf_op jit(solution)/shard_map/psum | solution.py:67
  564.0 102.5 %while.68 = (s32[]{:T(128)}, f32[2048]{0:T(1024)S(1)}, f32[16,256]{1,0:T(8,128)S(1)}, s32[16]{0:T(128)S(1)}, bf16[64,4096]{1,0:T(8,128)(2,1)S(1)}, /*index=5*/bf...) while((s32[]{:T(128)}, f32[2048]{0:T(1024)S(1)}, ...), condition=%wide.region_28.29_spmd.clone, body=%wide.region_27.28_spmd.clone.sunk | while | flops 81793032 | bytes 6644961 | solution.py:37
  619.9 1.7 fusion.152
  666.5 5.8 psum.137
  673.6 27.5 %psum.138 = f32[4096]{0:T(1024)S(1)} all-reduce(f32[4096]{0:T(1024)S(1)} %bitcast.179), channel_id=1, replica_groups=mesh['work'=8,'firm'=4] {'work'}, use_global_device_ids=true, to_apply=%region_31.32 | all-reduce | flops 4096 | bytes 32768 | tf_op jit(solution)/shard_map/psum | solution.py:42
  703.8 46.4 %all-reduce.1 = (f32[]{:T(128)}, f32[]{:T(128)}) all-reduce(f32[]{:T(128)S(6)} %add.206, f32[]{:T(128)S(6)} %add.209), channel_id=1, replica_groups=mesh['work'=8,'firm'=4] {'work','firm'}, use_global_device_ids=true, to_apply=%region_26.27 | all-reduce | flops 2 | bytes 16 | tf_op jit(solution)/shard_map/psum | solution.py:67
  754.1 104.5 %while.69 = (s32[]{:T(128)}, f32[2048]{0:T(1024)S(1)}, f32[16,256]{1,0:T(8,128)S(1)}, s32[16]{0:T(128)S(1)}, bf16[64,4096]{1,0:T(8,128)(2,1)S(1)}, /*index=5*/bf...) while((s32[]{:T(128)}, f32[2048]{0:T(1024)S(1)}, ...), condition=%wide.region_38.39_spmd.clone, body=%wide.region_37.38_spmd.clone.sunk | while | flops 81793032 | bytes 6644961 | solution.py:37
  858.5 5.8 psum.141
  865.7 27.5 %psum.142 = f32[4096]{0:T(1024)S(1)} all-reduce(f32[4096]{0:T(1024)S(1)} %bitcast.180), channel_id=1, replica_groups=mesh['work'=8,'firm'=4] {'work'}, use_global_device_ids=true, to_apply=%region_41.42 | all-reduce | flops 4096 | bytes 32768 | tf_op jit(solution)/shard_map/psum | solution.py:42
  895.8 46.5 %all-reduce = (f32[]{:T(128)}, f32[]{:T(128)}) all-reduce(f32[]{:T(128)S(6)} %add.214, f32[]{:T(128)S(6)} %add.217), channel_id=1, replica_groups=mesh['work'=8,'firm'=4] {'work','firm'}, use_global_device_ids=true, to_apply=%region_36.37 | all-reduce | flops 2 | bytes 16 | tf_op jit(solution)/shard_map/psum | solution.py:67
  (655 shorter events, 449.0 us)
Async XLA Ops:
  36.3 135.4 %copy-start = (s32[4096]{0:T(1024)S(1)}, s32[4096]{0:T(1024)}, u32[]{:S(2)}) copy-start(s32[4096]{0:T(1024)} %param.21) | copy-start | bytes 49156
  36.3 141.9 %copy-start.1 = (s32[2048]{0:T(1024)S(1)}, s32[2048]{0:T(1024)}, u32[]{:S(2)}) copy-start(s32[2048]{0:T(1024)} %param.20) | copy-start | bytes 24580
where the time goes:
time: 957 us; the launch traced here: 948 us
  blocking collectives  399 us (42%)
  matrix products  340 us (36%)
  local copies, waits for them, and re-layouts  120 us (13%)
  loops' own time  55.9 us (6%)
  between operations  24.8 us (3%)
    psum x4, blocking collectives, two_products(): lax.psum((local_dot(left_u, left_v, left_u, left_v), local_dot(left_u, le...  183 us
    psum x5, blocking collectives, kernel_pass(): cols = lax.psum(cols_part, 'work')  151 us
    dot_general x80, matrix products, step(): col_blk = jnp.dot(vec_u, kernel, precision=lax.Precision.HIGHEST)  138 us
    dot_general x80, matrix products, step(): lax.dot_general(wfeat, feat_blk, (((0,), (0,)), ((), ())), preferred_elem...  106 us
    dot_general x80, matrix products, step(): jnp.dot(kernel, vec_blk, precision=lax.Precision.HIGHEST)  94.9 us
    dynamic_slice x80, local copies, waits for them, and re-layouts, step(): pot_blk = lax.dynamic_slice_in_dim(firm_pot, start, width, 0)  61.2 us
    another operation x5, loops' own time, kernel_pass(): lax.scan(step, jnp.zeros((rows_here,), jnp.float32), jnp.arange(blocks, d...  55.9 us
    dynamic_slice x80, local copies, waits for them, and re-layouts, kernel_pass(): lax.scan(step, jnp.zeros((rows_here,), jnp.float32), jnp.arange(blocks, d...  50.6 us

commit v1 on v0

--- a/solution.py
+++ b/solution.py
@@ -7,9 +7,30 @@
 ITERS = 4
 
 
+def ring_gather(x, axis, dim):
+    peers, position, rows = (lax.axis_size(axis), lax.axis_index(axis), x.shape[dim])
+    ahead = [(i, (i + 1) % peers) for i in range(peers)]
+    left = [(i, (i - 1) % peers) for i in range(peers)]
+    filled = jnp.zeros((*x.shape[:dim], peers * rows, *x.shape[dim + 1 :]), x.dtype)
+    filled = lax.dynamic_update_slice_in_dim(filled, x, position * rows, axis=dim)
+    from_left = from_right = x
+    halfway = peers // 2
+    for step in range(1, halfway + 1):
+        from_left = lax.ppermute(from_left, axis, ahead)
+        filled = lax.dynamic_update_slice_in_dim(
+            filled, from_left, (position - step) % peers * rows, axis=dim
+        )
+        if step < peers - halfway:
+            from_right = lax.ppermute(from_right, axis, left)
+            filled = lax.dynamic_update_slice_in_dim(
+                filled, from_right, (position + step) % peers * rows, axis=dim
+            )
+    return filled
+
+
 def body(worker_feat, firm_feat, worker_pot, firm_pot, worker_caps, firm_caps):
     wfeat = lax.all_gather(worker_feat, "firm", axis=0, tiled=True)
-    ffeat = lax.all_gather(firm_feat, "work", axis=0, tiled=True)
+    ffeat = ring_gather(firm_feat, "work", 0)
     rows_here = wfeat.shape[1]
     cols_here = ffeat.shape[1]
     inverse = 1.0 / (cols_here * lax.axis_size("firm"))

time: 957 us -> 827 us (0.86)
  matrix products: 340 us -> 284 us
  local copies, waits for them, and re-layouts: 120 us -> 65.3 us
  blocking collectives: 399 us -> 372 us
  starting transfers between devices: 0 us -> 11.6 us
    dot_general x80, matrix products: 106 us -> 51.3 us  [step(): lax.dot_general(wfeat, feat_blk, (((0,), (0,)), ((), ())), preferred_elem...]
    dynamic_slice x80, local copies, waits for them, and re-layouts: 61.2 us -> 6.3 us  [step(): pot_blk = lax.dynamic_slice_in_dim(firm_pot, start, width, 0)]
    all_gather x1 -> x0, blocking collectives: 29.7 us -> none  [body(): ffeat = lax.all_gather(firm_feat, 'work', axis=0, tiled=True)]
    ppermute x0 -> x7, starting transfers between devices: none -> 11.6 us  [the longest x4 10.8 us: ring_gather(): from_left = lax.ppermute(from_left, axis, ahead)]
  transfers between devices with their start and end apart: 0 -> 7, of which waited for: 0 -> 3; matrix products, arithmetic and copies ran while one was open for 0% -> 0% of each run, Pallas kernels for 0% -> 0%
where the time goes in v1:
time: 827 us; the launch traced here: 824 us
  blocking collectives  372 us (45%)
  matrix products  284 us (34%)
  local copies, waits for them, and re-layouts  65.3 us (8%)
  loops' own time  53.9 us (7%)
  between operations  24.8 us (3%)
  starting transfers between devices  11.6 us (1%)
    psum x4, blocking collectives, two_products(): lax.psum((local_dot(left_u, left_v, left_u, left_v), local_dot(left_u, le...  183 us
    psum x5, blocking collectives, kernel_pass(): cols = lax.psum(cols_part, 'work')  153 us
    dot_general x80, matrix products, step(): col_blk = jnp.dot(vec_u, kernel, precision=lax.Precision.HIGHEST)  138 us
    dot_general x80, matrix products, step(): jnp.dot(kernel, vec_blk, precision=lax.Precision.HIGHEST)  94.9 us
    another operation x5, loops' own time, kernel_pass(): lax.scan(step, jnp.zeros((rows_here,), jnp.float32), jnp.arange(blocks, d...  53.9 us
    dot_general x80, matrix products, step(): lax.dot_general(wfeat, feat_blk, (((0,), (0,)), ((), ())), preferred_elem...  51.3 us
    dynamic_slice x80, local copies, waits for them, and re-layouts, kernel_pass(): lax.scan(step, jnp.zeros((rows_here,), jnp.float32), jnp.arange(blocks, d...  49.9 us
    psum x5, blocking collectives, kernel_pass(): rows_full = lax.psum(rows_part, 'firm')  29.8 us
  transfers between devices with their start and end apart: 7, of which 3 were waited for; matrix products, arithmetic and copies ran while one was open for 0% of the time, Pallas kernels for 0%

profile of v1, /device:TPU:12, one launch (start us, length us, event | category | flops | bytes accessed | tf_op | source)
XLA Modules:
  0.0 824.3 jit_solution(3296113879459534357)
XLA Ops:
  3.6 6.0 all_gather.3
  9.6 2.4 collective-permute-start.2
  12.1 1.9 collective-permute-done.2
  14.0 3.4 collective-permute-start.4
  19.3 3.4 collective-permute-start.6
  22.7 1.9 collective-permute-done.6
  24.6 79.5 %while.65 = (s32[]{:T(128)}, f32[2048]{0:T(1024)S(1)}, f32[16,256]{1,0:T(8,128)S(1)}, s32[16]{0:T(128)S(1)}, bf16[64,4096]{1,0:T(8,128)(2,1)S(1)}, /*index=5*/bf...) while((s32[]{:T(128)}, f32[2048]{0:T(1024)S(1)}, ...), condition=%wide.region_1.2_spmd.clone, body=%wide.region_0.1_spmd.clone.sunk | while | flops 81793032 | bytes 6633677 | solution.py:58
  104.2 37.4 %psum.127 = f32[4096]{0:T(1024)S(1)} all-reduce(f32[4096]{0:T(1024)S(1)} %bitcast.176), channel_id=1, replica_groups=mesh['work'=8,'firm'=4] {'work'}, use_global_device_ids=true, to_apply=%region_4.5 | all-reduce | flops 4096 | bytes 32768 | tf_op jit(solution)/shard_map/psum | solution.py:63
  141.6 5.7 psum.126
  147.4 80.8 %while.66 = (s32[]{:T(128)}, f32[2048]{0:T(1024)S(1)}, f32[16,256]{1,0:T(8,128)S(1)}, s32[16]{0:T(128)S(1)}, bf16[64,4096]{1,0:T(8,128)(2,1)S(1)}, /*index=5*/bf...) while((s32[]{:T(128)}, f32[2048]{0:T(1024)S(1)}, ...), condition=%wide.region_8.9_spmd.clone, body=%wide.region_7.8_spmd.clone.sunk | while | flops 81793032 | bytes 6644961 | solution.py:58
  150.7 1.7 fusion.134
  155.7 1.7 fusion.134
  160.8 1.7 fusion.134
  165.8 1.7 fusion.134
  170.9 1.7 fusion.134
  228.2 6.7 psum.129
  234.9 33.0 %psum.130 = f32[4096]{0:T(1024)S(1)} all-reduce(f32[4096]{0:T(1024)S(1)} %bitcast.177), channel_id=1, replica_groups=mesh['work'=8,'firm'=4] {'work'}, use_global_device_ids=true, to_apply=%region_11.12 | all-reduce | flops 4096 | bytes 32768 | tf_op jit(solution)/shard_map/psum | solution.py:63
  271.7 43.5 %all-reduce.3 = (f32[]{:T(128)}, f32[]{:T(128)}) all-reduce(f32[]{:T(128)S(6)} %add.271, f32[]{:T(128)S(6)} %add.274), channel_id=1, replica_groups=mesh['work'=8,'firm'=4] {'work','firm'}, use_global_device_ids=true, to_apply=%region_6.7 | all-reduce | flops 2 | bytes 16 | tf_op jit(solution)/shard_map/psum | solution.py:88
  316.5 81.3 %while.67 = (s32[]{:T(128)}, f32[2048]{0:T(1024)S(1)}, f32[16,256]{1,0:T(8,128)S(1)}, s32[16]{0:T(128)S(1)}, bf16[64,4096]{1,0:T(8,128)(2,1)S(1)}, /*index=5*/bf...) while((s32[]{:T(128)}, f32[2048]{0:T(1024)S(1)}, ...), condition=%wide.region_18.19_spmd.clone, body=%wide.region_17.18_spmd.clone.sunk | while | flops 81793032 | bytes 6644961 | solution.py:58
  319.8 1.7 fusion.143
  397.9 5.8 psum.133
  404.4 27.5 %psum.134 = f32[4096]{0:T(1024)S(1)} all-reduce(f32[4096]{0:T(1024)S(1)} %bitcast.178), channel_id=1, replica_groups=mesh['work'=8,'firm'=4] {'work'}, use_global_device_ids=true, to_apply=%region_21.22 | all-reduce | flops 4096 | bytes 32768 | tf_op jit(solution)/shard_map/psum | solution.py:63
  435.1 46.5 %all-reduce.2 = (f32[]{:T(128)}, f32[]{:T(128)}) all-reduce(f32[]{:T(128)S(6)} %add.275, f32[]{:T(128)S(6)} %add.278), channel_id=1, replica_groups=mesh['work'=8,'firm'=4] {'work','firm'}, use_global_device_ids=true, to_apply=%region_16.17 | all-reduce | flops 2 | bytes 16 | tf_op jit(solution)/shard_map/psum | solution.py:88
  486.1 79.0 %while.68 = (s32[]{:T(128)}, f32[2048]{0:T(1024)S(1)}, f32[16,256]{1,0:T(8,128)S(1)}, s32[16]{0:T(128)S(1)}, bf16[64,4096]{1,0:T(8,128)(2,1)S(1)}, /*index=5*/bf...) while((s32[]{:T(128)}, f32[2048]{0:T(1024)S(1)}, ...), condition=%wide.region_28.29_spmd.clone, body=%wide.region_27.28_spmd.clone.sunk | while | flops 81793032 | bytes 6644961 | solution.py:58
  514.0 1.7 fusion.152
  565.2 5.8 psum.137
  571.6 27.5 %psum.138 = f32[4096]{0:T(1024)S(1)} all-reduce(f32[4096]{0:T(1024)S(1)} %bitcast.179), channel_id=1, replica_groups=mesh['work'=8,'firm'=4] {'work'}, use_global_device_ids=true, to_apply=%region_31.32 | all-reduce | flops 4096 | bytes 32768 | tf_op jit(solution)/shard_map/psum | solution.py:63
  602.3 46.6 %all-reduce.1 = (f32[]{:T(128)}, f32[]{:T(128)}) all-reduce(f32[]{:T(128)S(6)} %add.283, f32[]{:T(128)S(6)} %add.286), channel_id=1, replica_groups=mesh['work'=8,'firm'=4] {'work','firm'}, use_global_device_ids=true, to_apply=%region_26.27 | all-reduce | flops 2 | bytes 16 | tf_op jit(solution)/shard_map/psum | solution.py:88
  652.9 82.5 %while.69 = (s32[]{:T(128)}, f32[2048]{0:T(1024)S(1)}, f32[16,256]{1,0:T(8,128)S(1)}, s32[16]{0:T(128)S(1)}, bf16[64,4096]{1,0:T(8,128)(2,1)S(1)}, /*index=5*/bf...) while((s32[]{:T(128)}, f32[2048]{0:T(1024)S(1)}, ...), condition=%wide.region_38.39_spmd.clone, body=%wide.region_37.38_spmd.clone.sunk | while | flops 81793032 | bytes 6644961 | solution.py:58
  735.4 5.8 psum.141
  741.9 27.5 %psum.142 = f32[4096]{0:T(1024)S(1)} all-reduce(f32[4096]{0:T(1024)S(1)} %bitcast.180), channel_id=1, replica_groups=mesh['work'=8,'firm'=4] {'work'}, use_global_device_ids=true, to_apply=%region_41.42 | all-reduce | flops 4096 | bytes 32768 | tf_op jit(solution)/shard_map/psum | solution.py:63
  772.6 46.5 %all-reduce = (f32[]{:T(128)}, f32[]{:T(128)}) all-reduce(f32[]{:T(128)S(6)} %add.291, f32[]{:T(128)S(6)} %add.294), channel_id=1, replica_groups=mesh['work'=8,'firm'=4] {'work','firm'}, use_global_device_ids=true, to_apply=%region_36.37 | all-reduce | flops 2 | bytes 16 | tf_op jit(solution)/shard_map/psum | solution.py:88
  (681 shorter events, 348.7 us)
Async XLA Ops:
  0.6 24.0 %copy-start.3 = (f32[2048]{0:T(1024)S(1)}, f32[2048]{0:T(1024)}, u32[]{:S(2)}) copy-start(f32[2048]{0:T(1024)} %param.18) | copy-start | bytes 24580
  0.6 24.0 %copy-start = (f32[4096]{0:T(1024)S(1)}, f32[4096]{0:T(1024)}, u32[]{:S(2)}) copy-start(f32[4096]{0:T(1024)} %param.19) | copy-start | bytes 49156
  0.6 9.0 %collective-permute-start = (bf16[8,4096]{1,0:T(8,128)(2,1)}, bf16[8,4096]{1,0:T(8,128)(2,1)S(1)}, u32[]{:S(2)}, u32[]{:S(2)}) collective-permute-start(bf16[8,4096]{1,0:T(8,128)(2,1)} %param.17), channel_id=1, source_target_pairs={{0,4},{4,8},{8,12},{12,16},{16,20},{20,24},{24,28},{28,0},{1,5},{5... | collective-permute-start | bytes 196616 | tf_op jit(solution)/shard_map/ppermute | solution.py:19
  2.2 9.8 %collective-permute-start.1 = (bf16[8,4096]{1,0:T(8,128)(2,1)}, bf16[8,4096]{1,0:T(8,128)(2,1)S(1)}, u32[]{:S(2)}, u32[]{:S(2)}) collective-permute-start(bf16[8,4096]{1,0:T(8,128)(2,1)} %param.17), channel_id=1, source_target_pairs={{0,28},{4,0},{8,4},{12,8},{16,12},{20,16},{24,20},{28,24},{1,29},{... | collective-permute-start | bytes 196616 | tf_op jit(solution)/shard_map/ppermute | solution.py:24
  9.6 4.3 collective-permute-start.2
  12.1 5.3 collective-permute-start.3
  14.0 5.3 collective-permute-start.4
  17.4 5.3 collective-permute-start.5
  19.3 5.3 collective-permute-start.6
  24.6 122.7 %copy-start.1 = (s32[4096]{0:T(1024)S(1)}, s32[4096]{0:T(1024)}, u32[]{:S(2)}) copy-start(s32[4096]{0:T(1024)} %param.21) | copy-start | bytes 49156
  24.6 122.7 %copy-start.2 = (s32[2048]{0:T(1024)S(1)}, s32[2048]{0:T(1024)}, u32[]{:S(2)}) copy-start(s32[2048]{0:T(1024)} %param.20) | copy-start | bytes 24580
